TPU v7x, 256 devices: a whole 4x4x8 slice. The times are simulated.
256 devices in a mesh: row: 8 (over y, x_lo), col: 32 (over z, x_hi, core).
Axes of the slice: x: 4 (x_hi: 2, x_lo: 2; x = x_hi * 2 + x_lo), y: 4, z: 8, core: 2. Of those that a mesh axis runs over, the one named last changes fastest.
Arguments:
- blocks: bfloat16 [32, 4096, 8192], P('row', 'col'), may hold values from -1800 to 1800, as said below
- factor_b: float32 [8192, 256], P('col'), may hold values from -6 to 6
- factor_c: float32 [64, 256], replicated, may hold values from -0.75 to 0.75
- block_pos: int32 [32, 32], P('row', 'col'), may hold values from 0 to 7, as said below
- block_count: int32 [8, 32], P('row', 'col'), may hold values from 1 to 4, as said below
Outputs:
- factor_a_new: float32 [4096, 256], P(('row', 'col'))
- factor_b_new: float32 [8192, 256], P(('col', 'row'))
Inputs may be any that keep to these rules, and one draw needn't show every extreme that they name: `blocks`: every entry is finite. `block_pos`: the 4 positions of one device are distinct. `block_count`: some device has all 4 slots live.
All inputs are finite; a program needn't handle non-finite values.
Results may differ from a plain program's by a relative error of at most 0.007.
Values may be sent and summed in bfloat16 or wider, within the bound.
A program may use at most 64 MiB of HBM per device.

v0:
```python
import jax
import jax.numpy as jnp
from jax import lax
from jax.sharding import PartitionSpec as P

IB_DEV = 4
JB_DEV = 2
norm_eps = 1e-06


def solve_right(rows_in, matrix):
    lower = jnp.linalg.cholesky(matrix)
    half = lax.linalg.triangular_solve(
        lower, rows_in, left_side=False, lower=True, transpose_a=True
    )
    return lax.linalg.triangular_solve(lower, half, left_side=False, lower=True, transpose_a=False)


def body(blocks, factor_b, factor_c, block_pos, block_count):
    high = lax.Precision.HIGHEST
    tile_side = blocks.shape[1]
    depth = factor_c.shape[0]
    rank_width = factor_c.shape[1]
    col_slab = factor_b.shape[0]
    row_slab = IB_DEV * tile_side
    live_count = block_count[0, 0]
    positions = block_pos[:, 0]
    c_low = factor_c.astype(jnp.bfloat16)
    b_low = factor_b.astype(jnp.bfloat16)
    gram_c = jnp.dot(factor_c.T, factor_c, precision=high)
    gram_b = lax.psum(jnp.dot(factor_b.T, factor_b, precision=high), "col")
    v_one = gram_b * gram_c

    def cube_of(index):
        tile = lax.dynamic_index_in_dim(blocks, index, 0, keepdims=False)
        return tile.reshape(tile_side, tile_side, depth)

    def first_term(cube, b_tile):
        inner = lax.dot_general(
            cube, c_low, (((2,), (0,)), ((), ())), preferred_element_type=jnp.float32
        )
        return jnp.sum(inner * b_tile.astype(jnp.float32)[None], axis=1)

    def second_term(cube, a_tile):
        inner = lax.dot_general(
            cube, c_low, (((2,), (0,)), ((), ())), preferred_element_type=jnp.float32
        )
        return jnp.sum(inner * a_tile.astype(jnp.float32)[:, None, :], axis=0)

    def mode_one(index, total):
        place = positions[index]
        b_tile = lax.dynamic_slice_in_dim(b_low, place % JB_DEV * tile_side, tile_side, 0)
        term = first_term(cube_of(index), b_tile)
        start = place // JB_DEV * tile_side
        old = lax.dynamic_slice_in_dim(total, start, tile_side, 0)
        return lax.dynamic_update_slice_in_dim(total, old + term, start, 0)

    partial_a = lax.fori_loop(
        0, live_count, mode_one, jnp.zeros((row_slab, rank_width), jnp.float32)
    )
    rows_total = row_slab * lax.axis_size("row")
    share_rows = row_slab // lax.axis_size("col")
    sum_a = lax.psum(partial_a, "col")
    new_full = solve_right(sum_a, v_one)
    gram_a = lax.psum(jnp.dot(new_full.T, new_full, precision=high), "row")
    scale_a = jnp.sqrt(jnp.diagonal(gram_a) / rows_total + norm_eps)
    hat_full = new_full / scale_a[None, :]
    slab_low = hat_full.astype(jnp.bfloat16)
    hat_a = lax.dynamic_slice_in_dim(hat_full, lax.axis_index("col") * share_rows, share_rows, 0)
    v_two = gram_a / (scale_a[:, None] * scale_a[None, :]) * gram_c

    def mode_two(index, total):
        place = positions[index]
        a_tile = lax.dynamic_slice_in_dim(slab_low, place // JB_DEV * tile_side, tile_side, 0)
        term = second_term(cube_of(index), a_tile)
        start = place % JB_DEV * tile_side
        old = lax.dynamic_slice_in_dim(total, start, tile_side, 0)
        return lax.dynamic_update_slice_in_dim(total, old + term, start, 0)

    partial_b = lax.fori_loop(
        0, live_count, mode_two, jnp.zeros((col_slab, rank_width), jnp.float32)
    )
    part_b = lax.psum_scatter(partial_b, "row", scatter_dimension=0, tiled=True)
    new_b = solve_right(part_b, v_two)
    squares_b = lax.psum(jnp.sum(new_b * new_b, axis=0), ("row", "col"))
    scale_b = jnp.sqrt(squares_b / (col_slab * lax.axis_size("col")) + norm_eps)
    hat_b = new_b / scale_b[None, :]
    return (hat_a, hat_b)


def solution(mesh):
    return jax.shard_map(
        body,
        mesh=mesh,
        in_specs=(P("row", "col", None), P("col", None), P(), P("row", "col"), P("row", "col")),
        out_specs=(P(("row", "col"), None), P(("col", "row"), None)),
        check_vma=False,
    )
```

profile of v0, /device:TPU:1, one launch (start us, length us, event | category | flops | bytes accessed | tf_op | source)
XLA Modules:
  0.0 723.0 jit_solution(14343702082353428203)
XLA Ops:
  7.2 1.0 convert_element_type.22
  8.2 2.3 fusion.33
  10.5 12.0 %copy.17 = bf16[4,128,8192]{1,2,0:T(8,128)(2,1)} copy(bf16[4,128,8192]{2,1,0:T(8,128)(2,1)} %param.10) | data formatting | bytes 16777216 | tf_op jit(solution)/shard_map/while | solution.py:58
  22.5 26.2 %while.26 = (s32[]{:T(128)}, f32[512,256]{1,0:T(8,128)S(1)}, s32[]{:T(128)}, s32[4]{0:T(128)S(1)}, bf16[4,128,8192]{1,2,0:T(8,128)(2,1)}, /*index=5*/bf16[64,256...) while((s32[]{:T(128)}, f32[512,256]{1,0:T(8,128)S(1)}, ...), condition=%wide.region_2.3_spmd, body=%wide.region_0.2_spmd.sunk | while | flops 545292288 | bytes 11370982 | solution.py:58
  23.2 0.6 dynamic_slice.71
  26.1 1.7 constant_dynamic-slice_fusion.11
  27.8 3.5 copy.34
  31.3 4.0 multiply_reduce_fusion.5
  36.0 0.6 dynamic_slice.71
  38.9 1.7 constant_dynamic-slice_fusion.11
  40.6 3.5 copy.34
  44.1 4.0 multiply_reduce_fusion.5
  48.8 0.9 copy-done.1
  49.7 0.4 all-reduce.5.cloned.1.call-start
  50.1 300.5 %all-reduce.7.cloned.1.call-done = (f32[512,256]{1,0:T(8,128)}, f32[256,256]{0,1:T(8,128)}) async-done(((f32[512,256]{1,0:T(8,128)}, f32[256,256]{0,1:T(8,128)}), (f32[512,256]{1,0:T(8,128)}, f32[256,256]{0,1:T(8,128)})) %all-reduce.7.cloned.1.call-update) | async-done | bytes 786448 | tf_op jit(solution)/shard_map/psum | solution.py:63
  350.6 1.4 fusion.32
  352.2 11.7 %cholesky.130 = f32[128,128]{1,0:T(8,128)S(1)} custom-call(f32[128,128]{1,0:T(8,128)S(1)} %cholesky.194), custom_call_target="Cholesky" | custom-call | tf_op jit(solution)/shard_map/jit(cholesky)/cholesky | solution.py:12
  364.0 9.8 %custom-call.23 = f32[1,128,128]{1,2,0:T(8,128)S(1)} custom-call(f32[1,128,128]{2,1,0:T(8,128)S(1)} %get-tuple-element.295), custom_call_target="InvertDiagBlocksLowerTriangular" | custom-call | tf_op jit(solution)/shard_map/jit(cholesky)/cholesky | solution.py:12
  374.0 0.3 convolution_subtract_fusion.3
  374.3 11.7 %cholesky.147 = f32[128,128]{1,0:T(8,128)S(1)} custom-call(f32[128,128]{1,0:T(8,128)S(1)} %convolution_subtract_fusion.3), custom_call_target="Cholesky" | custom-call | tf_op jit(solution)/shard_map/jit(cholesky)/cholesky | solution.py:12
  386.0 0.7 compare_reduce_fusion.2
  388.1 15.6 %while.28 = (s32[]{:T(128)}, f32[256,256]{1,0:T(8,128)S(1)}, s32[2,2]{1,0:T(2,128)S(1)}, f32[2,128,128]{2,1,0:T(8,128)S(1)}, s32[]{:T(128)}) while((s32[]{:T(128)}, f32[256,256]{1,0:T(8,128)S(1)}, s32[2,2]{1,0:T(2,128)S(1)}, f32[2,128,128]{2,1,0:T(8,128)S(1)}, s32[]{:T(128)}) %tuple.97), condition=%wide.while_cond, body=%wide.while_body.sunk | while | flops 2 | bytes 131189 | solution.py:13
  399.8 0.6 fusion.64
  400.4 1.4 bitcast_dynamic-update-slice_fusion.4
  401.8 0.6 fusion.64
  402.4 1.4 bitcast_dynamic-update-slice_fusion.4
  403.7 19.7 %custom-call.18 = f32[2,128,128]{1,2,0:T(8,128)S(1)} custom-call(f32[2,128,128]{2,1,0:T(8,128)S(1)} %get-tuple-element.202), custom_call_target="InvertDiagBlocksLowerTriangular" | custom-call | tf_op jit(solution)/shard_map/triangular_solve | solution.py:13
  423.4 0.4 fusion.4
  423.8 0.4 convolution_subtract_fusion.1
  424.2 0.4 fusion.16
  424.6 0.4 fusion.15
  425.0 0.6 convolution_subtract_fusion
  425.6 0.4 fusion.14
  425.9 1.3 fusion.3
  427.4 73.3 %all-reduce.5.cloned.1.call-done = f32[256,256]{0,1:T(8,128)} async-done(((f32[256,256]{0,1:T(8,128)}), f32[256,256]{0,1:T(8,128)}) %all-reduce.5.cloned.1.call-update) | async-done | bytes 262160 | tf_op jit(solution)/shard_map/psum | solution.py:65
  500.7 2.7 gather_fusion
  503.6 0.7 copy.26
  504.6 11.7 %cholesky.164 = f32[128,128]{1,0:T(8,128)S(1)} custom-call(f32[128,128]{1,0:T(8,128)S(1)} %cholesky.197), custom_call_target="Cholesky" | custom-call | tf_op jit(solution)/shard_map/jit(cholesky)/cholesky | solution.py:12
  516.4 9.8 %custom-call.24 = f32[1,128,128]{1,2,0:T(8,128)S(1)} custom-call(f32[1,128,128]{2,1,0:T(8,128)S(1)} %get-tuple-element.291), custom_call_target="InvertDiagBlocksLowerTriangular" | custom-call | tf_op jit(solution)/shard_map/jit(cholesky)/cholesky | solution.py:12
  526.4 0.3 convolution_subtract_fusion.2
  526.7 11.7 %cholesky.181 = f32[128,128]{1,0:T(8,128)S(1)} custom-call(f32[128,128]{1,0:T(8,128)S(1)} %convolution_subtract_fusion.2), custom_call_target="Cholesky" | custom-call | tf_op jit(solution)/shard_map/jit(cholesky)/cholesky | solution.py:12
  538.4 0.7 compare_reduce_fusion.1
  539.1 0.6 compare_reduce_fusion
  539.8 28.4 %while.27 = (s32[]{:T(128)}, f32[256,256]{1,0:T(8,128)S(1)}, s32[]{:T(128)}, s32[4]{0:T(128)S(1)}, bf16[4,128,8192]{1,2,0:T(8,128)(2,1)}, /*index=5*/bf16[64,256...) while((s32[]{:T(128)}, f32[256,256]{1,0:T(8,128)S(1)}, ...), condition=%wide.region_12.14_spmd, body=%wide.region_10.13_spmd.sunk | while | flops 545292288 | bytes 11633126 | solution.py:80
  540.6 0.6 dynamic_slice.75
  543.1 1.7 constant_dynamic-slice_fusion.12
  544.8 3.5 copy.35
  549.1 4.6 multiply_reduce_fusion.6
  554.4 0.6 dynamic_slice.75
  556.9 1.7 constant_dynamic-slice_fusion.12
  558.6 3.5 copy.35
  562.9 4.6 multiply_reduce_fusion.6
  568.2 0.7 copy-done.2
  570.2 3.9 while.29
  570.2 0.6 fusion.65
  570.8 1.3 bitcast_dynamic-update-slice_fusion.5
  572.2 0.6 fusion.65
  572.8 1.3 bitcast_dynamic-update-slice_fusion.5
  574.1 19.7 %custom-call.19 = f32[2,128,128]{1,2,0:T(8,128)S(1)} custom-call(f32[2,128,128]{2,1,0:T(8,128)S(1)} %get-tuple-element.210), custom_call_target="InvertDiagBlocksLowerTriangular" | custom-call | tf_op jit(solution)/shard_map/triangular_solve | solution.py:13
  593.8 40.6 %reduce-scatter.2.cloned.1.call-done = f32[32,256]{1,0:T(8,128)} async-done(((f32[256,256]{1,0:T(8,128)}), f32[32,256]{1,0:T(8,128)}) %reduce-scatter.2.cloned.1.call-update) | async-done | bytes 32784 | tf_op jit(solution)/shard_map/reduce_scatter | solution.py:83
  634.4 0.9 fusion.18
  635.3 0.9 convolution_subtract_fusion.5
  637.0 78.5 %psum.31 = f32[256]{0:T(256)S(1)} all-reduce(f32[256]{0:T(256)S(1)} %multiply_reduce_fusion.2), channel_id=1, replica_groups=mesh['row'=8,'col'=32] {'row','col'}, use_global_device_ids=true, to_apply=%region_15.17 | all-reduce | flops 256 | bytes 2048 | tf_op jit(solution)/shard_map/psum | solution.py:85
  715.6 0.6 fusion.25
  (65 shorter events, 2.9 us)
Async XLA Ops:
  7.2 343.5 %all-reduce.7.cloned.1.call-start = ((), (), s32[]{:S(2)}) async-start(), calls=%async_computation.3 | async-start | bytes 1572864 | tf_op jit(solution)/shard_map/psum | solution.py:63
  10.5 12.0 %copy-start.3 = (f32[64,256]{1,0:T(8,128)S(1)}, f32[64,256]{1,0:T(8,128)}, u32[]{:S(2)}) copy-start(f32[64,256]{1,0:T(8,128)} %param.12) | copy-start | bytes 196612
  10.5 12.0 %copy-start.5 = (s32[4,1]{0,1:T(1,128)S(1)}, s32[4,1]{0,1:T(1,128)}, u32[]{:S(2)}) copy-start(s32[4,1]{0,1:T(1,128)} %param.13) | copy-start | bytes 52
  48.8 0.9 copy-start.1
  49.7 451.0 %all-reduce.5.cloned.1.call-start = ((), (), s32[]{:S(2)}) async-start(), calls=%async_computation.1 | async-start | bytes 524288 | tf_op jit(solution)/shard_map/psum | solution.py:65
  352.0 71.4 %copy-start.4 = (f32[512,256]{1,0:T(8,128)S(1)}, f32[512,256]{1,0:T(8,128)}, u32[]{:S(2)}) copy-start(f32[512,256]{1,0:T(8,128)} %get-tuple-element.280) | copy-start | bytes 1572868
  427.3 207.1 %reduce-scatter.2.cloned.1.call-start = ((), (), s32[]{:S(2)}) async-start(), calls=%async_computation.2 | async-start | bytes 294912 | tf_op jit(solution)/shard_map/reduce_scatter | solution.py:83
  500.7 3.6 copy-start
  568.2 0.7 copy-start.2
Sparse Core Ops, SparseCore 0:
  49.8 300.8 all-reduce.6
  427.4 73.2 all-reduce.4
  569.0 65.2 reduce-scatter.1
where the time goes:
time: 728 us; the launch traced here: 723 us
  waiting for transfers between devices  415 us (57%)
  other arithmetic  110 us (15%)
  blocking collectives  78.5 us (11%)
  local copies, waits for them, and re-layouts  48.6 us (7%)
  matrix products  28.2 us (4%)
  loops' own time  25.6 us (4%)
  between operations  16.9 us (2%)
    psum x1, waiting for transfers between devices, body(): sum_a = lax.psum(partial_a, 'col')  301 us
    psum x1, blocking collectives, body(): squares_b = lax.psum(jnp.sum(new_b * new_b, axis=0), ('row', 'col'))  78.5 us
    psum x1, waiting for transfers between devices, body(): gram_a = lax.psum(jnp.dot(new_full.T, new_full, precision=high), 'row')  73.3 us
    another operation x13, other arithmetic, solve_right(): lower = jnp.linalg.cholesky(matrix)  68.6 us
    reduce_scatter x1, waiting for transfers between devices, body(): part_b = lax.psum_scatter(partial_b, 'row', scatter_dimension=0, tiled=True)  40.6 us
    another operation x5, other arithmetic, solve_right(): lax.linalg.triangular_solve(lower, rows_in, left_side=False, lower=True,...  39.4 us
  transfers between devices with their start and end apart: 3, of which 3 were waited for; matrix products, arithmetic and copies ran while one was open for 3% of the time, Pallas kernels for 0%

commit v1 on v0

--- a/solution.py
+++ b/solution.py
@@ -82,7 +82,7 @@
     )
     part_b = lax.psum_scatter(partial_b, "row", scatter_dimension=0, tiled=True)
     new_b = solve_right(part_b, v_two)
-    squares_b = lax.psum(jnp.sum(new_b * new_b, axis=0), ("row", "col"))
+    squares_b = jnp.sum(lax.all_gather(jnp.sum(new_b * new_b, axis=0), ("row", "col")), axis=0)
     scale_b = jnp.sqrt(squares_b / (col_slab * lax.axis_size("col")) + norm_eps)
     hat_b = new_b / scale_b[None, :]
     return (hat_a, hat_b)

time: 728 us -> 1000 us (1.37)
  blocking collectives: 78.5 us -> 350 us
    all_gather x0 -> x1, blocking collectives: none -> 350 us  [body(): lax.all_gather(jnp.sum(new_b * new_b, axis=0), ('row', 'col'))]
    psum x1 -> x0, blocking collectives: 78.5 us -> none  [body(): squares_b = lax.psum(jnp.sum(new_b * new_b, axis=0), ('row', 'col'))]
  transfers between devices with their start and end apart: 3 -> 3, of which waited for: 3 -> 3; matrix products, arithmetic and copies ran while one was open for 3% -> 2% of each run, Pallas kernels for 0% -> 0%
where the time goes in v1:
time: 1000 us; the launch traced here: 995 us
  waiting for transfers between devices  415 us (42%)
  blocking collectives  350 us (35%)
  other arithmetic  110 us (11%)
  local copies, waits for them, and re-layouts  48.6 us (5%)
  matrix products  28.2 us (3%)
  loops' own time  25.6 us (3%)
  between operations  16.9 us (2%)
    all_gather x1, blocking collectives, body(): lax.all_gather(jnp.sum(new_b * new_b, axis=0), ('row', 'col'))  350 us
    psum x1, waiting for transfers between devices, body(): sum_a = lax.psum(partial_a, 'col')  301 us
    psum x1, waiting for transfers between devices, body(): gram_a = lax.psum(jnp.dot(new_full.T, new_full, precision=high), 'row')  73.3 us
    another operation x13, other arithmetic, solve_right(): lower = jnp.linalg.cholesky(matrix)  68.6 us
    reduce_scatter x1, waiting for transfers between devices, body(): part_b = lax.psum_scatter(partial_b, 'row', scatter_dimension=0, tiled=True)  40.6 us
    another operation x5, other arithmetic, solve_right(): lax.linalg.triangular_solve(lower, rows_in, left_side=False, lower=True,...  39.4 us
  transfers between devices with their start and end apart: 3, of which 3 were waited for; matrix products, arithmetic and copies ran while one was open for 2% of the time, Pallas kernels for 0%

profile of v1, /device:TPU:1, one launch (start us, length us, event | category | flops | bytes accessed | tf_op | source)
XLA Modules:
  0.0 994.7 jit_solution(11345057057398367608)
XLA Ops:
  7.2 1.0 convert_element_type.22
  8.2 2.3 fusion.33
  10.5 12.0 %copy.29 = bf16[4,128,8192]{1,2,0:T(8,128)(2,1)} copy(bf16[4,128,8192]{2,1,0:T(8,128)(2,1)} %param.10) | data formatting | bytes 16777216 | tf_op jit(solution)/shard_map/while | solution.py:58
  22.5 26.2 %while.26 = (s32[]{:T(128)}, f32[512,256]{1,0:T(8,128)S(1)}, s32[]{:T(128)}, s32[4]{0:T(128)S(1)}, bf16[4,128,8192]{1,2,0:T(8,128)(2,1)}, /*index=5*/bf16[64,256...) while((s32[]{:T(128)}, f32[512,256]{1,0:T(8,128)S(1)}, ...), condition=%wide.region_2.3_spmd, body=%wide.region_0.2_spmd.sunk | while | flops 545292288 | bytes 11370982 | solution.py:58
  23.2 0.6 dynamic_slice.71
  26.1 1.7 constant_dynamic-slice_fusion.11
  27.8 3.5 copy.46
  31.3 4.0 multiply_reduce_fusion.5
  36.0 0.6 dynamic_slice.71
  38.9 1.7 constant_dynamic-slice_fusion.11
  40.6 3.5 copy.46
  44.1 4.0 multiply_reduce_fusion.5
  48.8 0.9 copy-done.1
  49.7 0.4 all-reduce.5.cloned.1.call-start
  50.1 300.5 %all-reduce.7.cloned.1.call-done = (f32[512,256]{1,0:T(8,128)}, f32[256,256]{0,1:T(8,128)}) async-done(((f32[512,256]{1,0:T(8,128)}, f32[256,256]{0,1:T(8,128)}), (f32[512,256]{1,0:T(8,128)}, f32[256,256]{0,1:T(8,128)})) %all-reduce.7.cloned.1.call-update) | async-done | bytes 786448 | tf_op jit(solution)/shard_map/psum | solution.py:63
  350.6 1.4 fusion.32
  352.2 11.7 %cholesky.130 = f32[128,128]{1,0:T(8,128)S(1)} custom-call(f32[128,128]{1,0:T(8,128)S(1)} %cholesky.194), custom_call_target="Cholesky" | custom-call | tf_op jit(solution)/shard_map/jit(cholesky)/cholesky | solution.py:12
  364.0 9.8 custom-call.23
  374.3 11.7 %cholesky.147 = f32[128,128]{1,0:T(8,128)S(1)} custom-call(f32[128,128]{1,0:T(8,128)S(1)} %convolution_subtract_fusion.3), custom_call_target="Cholesky" | custom-call | tf_op jit(solution)/shard_map/jit(cholesky)/cholesky | solution.py:12
  386.0 0.7 compare_reduce_fusion.2
  388.1 15.6 %while.28 = (s32[]{:T(128)}, f32[256,256]{1,0:T(8,128)S(1)}, s32[2,2]{1,0:T(2,128)S(1)}, f32[2,128,128]{2,1,0:T(8,128)S(1)}, s32[]{:T(128)}) while((s32[]{:T(128)}, f32[256,256]{1,0:T(8,128)S(1)}, s32[2,2]{1,0:T(2,128)S(1)}, f32[2,128,128]{2,1,0:T(8,128)S(1)}, s32[]{:T(128)}) %tuple.100), condition=%wide.while_cond, body=%wide.while_body.sunk | while | flops 2 | bytes 131189 | solution.py:13
  399.8 0.6 fusion.64
  400.4 1.4 bitcast_dynamic-update-slice_fusion.4
  401.8 0.6 fusion.64
  402.4 1.4 bitcast_dynamic-update-slice_fusion.4
  403.7 19.7 %custom-call.18 = f32[2,128,128]{1,2,0:T(8,128)S(1)} custom-call(f32[2,128,128]{2,1,0:T(8,128)S(1)} %get-tuple-element.202), custom_call_target="InvertDiagBlocksLowerTriangular" | custom-call | tf_op jit(solution)/shard_map/triangular_solve | solution.py:13
  423.4 0.4 fusion.4
  423.8 0.4 convolution_subtract_fusion.1
  424.2 0.4 fusion.16
  424.6 0.4 fusion.15
  425.0 0.6 convolution_subtract_fusion
  425.6 0.4 fusion.14
  425.9 1.3 fusion.3
  427.4 73.3 %all-reduce.5.cloned.1.call-done = f32[256,256]{0,1:T(8,128)} async-done(((f32[256,256]{0,1:T(8,128)}), f32[256,256]{0,1:T(8,128)}) %all-reduce.5.cloned.1.call-update) | async-done | bytes 262160 | tf_op jit(solution)/shard_map/psum | solution.py:65
  500.7 2.7 gather_fusion
  503.6 0.7 copy.38
  504.6 11.7 %cholesky.164 = f32[128,128]{1,0:T(8,128)S(1)} custom-call(f32[128,128]{1,0:T(8,128)S(1)} %cholesky.197), custom_call_target="Cholesky" | custom-call | tf_op jit(solution)/shard_map/jit(cholesky)/cholesky | solution.py:12
  516.4 9.8 custom-call.24
  526.4 0.3 convolution_subtract_fusion.2
  526.7 11.7 %cholesky.181 = f32[128,128]{1,0:T(8,128)S(1)} custom-call(f32[128,128]{1,0:T(8,128)S(1)} %convolution_subtract_fusion.2), custom_call_target="Cholesky" | custom-call | tf_op jit(solution)/shard_map/jit(cholesky)/cholesky | solution.py:12
  538.4 0.7 compare_reduce_fusion.1
  539.1 0.6 compare_reduce_fusion
  539.8 28.4 %while.27 = (s32[]{:T(128)}, f32[256,256]{1,0:T(8,128)S(1)}, s32[]{:T(128)}, s32[4]{0:T(128)S(1)}, bf16[4,128,8192]{1,2,0:T(8,128)(2,1)}, /*index=5*/bf16[64,256...) while((s32[]{:T(128)}, f32[256,256]{1,0:T(8,128)S(1)}, ...), condition=%wide.region_12.14_spmd, body=%wide.region_10.13_spmd.sunk | while | flops 545292288 | bytes 11633126 | solution.py:80
  540.6 0.6 dynamic_slice.75
  543.1 1.7 constant_dynamic-slice_fusion.12
  544.8 3.5 copy.47
  549.1 4.6 multiply_reduce_fusion.6
  554.4 0.6 dynamic_slice.75
  556.9 1.7 constant_dynamic-slice_fusion.12
  558.6 3.5 copy.47
  562.9 4.6 multiply_reduce_fusion.6
  568.2 0.7 copy-done.2
  570.2 3.9 while.29
  570.2 0.6 fusion.65
  570.8 1.3 bitcast_dynamic-update-slice_fusion.5
  572.2 0.6 fusion.65
  572.8 1.3 bitcast_dynamic-update-slice_fusion.5
  574.1 19.7 %custom-call.19 = f32[2,128,128]{1,2,0:T(8,128)S(1)} custom-call(f32[2,128,128]{2,1,0:T(8,128)S(1)} %get-tuple-element.210), custom_call_target="InvertDiagBlocksLowerTriangular" | custom-call | tf_op jit(solution)/shard_map/triangular_solve | solution.py:13
  593.8 40.6 %reduce-scatter.2.cloned.1.call-done = f32[32,256]{1,0:T(8,128)} async-done(((f32[256,256]{1,0:T(8,128)}), f32[32,256]{1,0:T(8,128)}) %reduce-scatter.2.cloned.1.call-update) | async-done | bytes 32784 | tf_op jit(solution)/shard_map/reduce_scatter | solution.py:83
  634.4 0.9 fusion.18
  635.3 0.9 convolution_subtract_fusion.5
  637.0 350.0 %all-gather.1 = f32[256,1,256]{2,1,0:T(1,128)S(1)} all-gather(f32[1,1,256]{2,1,0:T(1,128)S(1)} %bitcast.111), channel_id=2, replica_groups=mesh['row'=8,'col'=32] {'row','col'}, dimensions={0}, use_global_device_ids=true | all-gather | bytes 263168 | tf_op jit(solution)/shard_map/all_gather | solution.py:85
  987.0 0.3 reduce_sum.43
  987.3 0.6 fusion.25
  (66 shorter events, 3.2 us)
Async XLA Ops:
  7.2 343.5 %all-reduce.7.cloned.1.call-start = ((), (), s32[]{:S(2)}) async-start(), calls=%async_computation.3 | async-start | bytes 1572864 | tf_op jit(solution)/shard_map/psum | solution.py:63
  10.5 12.0 %copy-start.3 = (f32[64,256]{1,0:T(8,128)S(1)}, f32[64,256]{1,0:T(8,128)}, u32[]{:S(2)}) copy-start(f32[64,256]{1,0:T(8,128)} %param.12) | copy-start | bytes 196612
  10.5 12.0 %copy-start.5 = (s32[4,1]{0,1:T(1,128)S(1)}, s32[4,1]{0,1:T(1,128)}, u32[]{:S(2)}) copy-start(s32[4,1]{0,1:T(1,128)} %param.13) | copy-start | bytes 52
  48.8 0.9 copy-start.1
  49.7 451.0 %all-reduce.5.cloned.1.call-start = ((), (), s32[]{:S(2)}) async-start(), calls=%async_computation.1 | async-start | bytes 524288 | tf_op jit(solution)/shard_map/psum | solution.py:65
  352.0 71.4 %copy-start.4 = (f32[512,256]{1,0:T(8,128)S(1)}, f32[512,256]{1,0:T(8,128)}, u32[]{:S(2)}) copy-start(f32[512,256]{1,0:T(8,128)} %get-tuple-element.296) | copy-start | bytes 1572868
  427.3 207.1 %reduce-scatter.2.cloned.1.call-start = ((), (), s32[]{:S(2)}) async-start(), calls=%async_computation.2 | async-start | bytes 294912 | tf_op jit(solution)/shard_map/reduce_scatter | solution.py:83
  500.7 3.6 copy-start
  568.2 0.7 copy-start.2
Sparse Core Ops, SparseCore 0:
  49.8 300.8 all-reduce.6
  427.4 73.2 all-reduce.4
  569.0 65.2 reduce-scatter.1
